TPU v7x, 512 devices: a whole 4x8x8 slice. The times are simulated.
512 devices in a mesh: dp: 16 (over y, core), expert: 32 (over z, x).
Axes of the slice: x: 4, y: 8, z: 8, core: 2. Of those that a mesh axis runs over, the one named last changes fastest.
Arguments:
- tokens: bfloat16 [65536, 2048], P(('dp', 'expert')), may hold values from -6 to 6
- out_grad: bfloat16 [65536, 2048], P(('dp', 'expert')), may hold values from -6 to 6
- route_ids: int32 [65536, 2], P(('dp', 'expert')), may hold values from 0 to 31, as said below
- route_gates: bfloat16 [65536, 2], P(('dp', 'expert')), may hold values from 0.049804688 to 1
- weight_in: bfloat16 [32, 2048, 512], P('expert', 'dp'), may hold values from -0.125 to 0.125
- weight_out: bfloat16 [32, 512, 2048], P('expert', None, 'dp'), may hold values from -0.25 to 0.25
Outputs:
- grad_tokens: bfloat16 [65536, 2048], P(('dp', 'expert'))
- grad_gates: bfloat16 [65536, 2], P(('dp', 'expert'))
- grad_weight_in: float32 [32, 2048, 512], P('expert', 'dp')
- grad_weight_out: float32 [32, 512, 2048], P('expert', None, 'dp')
Inputs may be any that keep to these rules, and one draw needn't show every extreme that they name: `route_ids`: each row names two different experts. Within the 128 tokens of one device (aligned blocks of 128 rows), every expert is named by at most 16 rows. For each index of dp, one expert is named by exactly 16 rows in every block of that index's 4096 rows.
All inputs are finite; a program needn't handle non-finite values.
Results may differ from a plain program's by a relative error of at most 0.017.
Values may be sent and summed in bfloat16 or wider, within the bound.
A program may use at most 64 MiB of HBM per device.

v0:
```python
import math

import jax
import jax.numpy as jnp
from jax import lax
from jax.sharding import PartitionSpec as P


def sent_together(arrays, axis, split_dim, concat_dim, along):
    widths = [math.prod(a.shape[along:]) for a in arrays]
    both = jnp.concatenate(
        [a.reshape(*a.shape[:along], w) for a, w in zip(arrays, widths)], axis=along
    )
    filled = lax.all_to_all(both, axis, split_axis=split_dim, concat_axis=concat_dim, tiled=True)
    tiles = jnp.split(filled, [sum(widths[:k]) for k in range(1, len(widths))], axis=along)
    return tuple(
        (b.reshape(*filled.shape[:along], *a.shape[along:]) for a, b in zip(arrays, tiles))
    )


def in_blocks(value, dim, devices):
    shape = value.shape
    tiles = value.reshape(*shape[:dim], devices, shape[dim] // devices, *shape[dim + 1 :])
    return jnp.moveaxis(tiles, dim, 0)


def sum_together(arrays, axis, dims):
    devices = lax.axis_size(axis)
    tiles = [in_blocks(a, dim, devices) for a, dim in zip(arrays, dims)]
    lines = jnp.concatenate([b.reshape(devices, -1) for b in tiles], axis=1)
    span = max(16, -(-lines.shape[1] // 1024) * 8)
    lines = jnp.pad(lines, ((0, 0), (0, span * 128 - lines.shape[1]))).reshape(-1, 128)
    ravelled, at, done = (lax.psum_scatter(lines, axis, tiled=True).reshape(-1), 0, [])
    for b in tiles:
        part = b[0]
        done.append(ravelled[at : at + part.size].reshape(part.shape))
        at += part.size
    return tuple(done)


def silu_slope(preact):
    logistic = jax.nn.sigmoid(preact)
    return logistic * (1.0 + preact * (1.0 - logistic))


def forward_rows(inputs, full_in):
    preact = jnp.dot(inputs, full_in, preferred_element_type=jnp.float32)
    return (preact, jax.nn.silu(preact).astype(jnp.bfloat16))


def backward_rows(inputs, grad_rows, gate_rows, preact, hidden_act, full_in, full_out):
    back_grad = lax.dot_general(
        grad_rows, full_out, (((1,), (1,)), ((), ())), preferred_element_type=jnp.float32
    )
    weight = gate_rows.astype(jnp.float32)[:, None]
    gate_grad = jnp.sum(hidden_act.astype(jnp.float32) * back_grad, axis=1)
    pre_grad = (weight * back_grad * silu_slope(preact)).astype(jnp.bfloat16)
    scaled = (weight * grad_rows.astype(jnp.float32)).astype(jnp.bfloat16)
    route_grad = lax.dot_general(
        pre_grad, full_in, (((1,), (1,)), ((), ())), preferred_element_type=jnp.float32
    ).astype(jnp.bfloat16)
    term_in = lax.dot_general(
        inputs, pre_grad, (((0,), (0,)), ((), ())), preferred_element_type=jnp.float32
    )
    term_out = lax.dot_general(
        hidden_act, scaled, (((0,), (0,)), ((), ())), preferred_element_type=jnp.float32
    )
    return (route_grad, gate_grad, term_in, term_out)


def on_device(tokens, out_grad, route_ids, route_gates, weight_in, weight_out):
    local_tokens, model_width = tokens.shape
    experts = lax.axis_size("expert")
    capacity = 4 * local_tokens // experts
    slot_count = experts * capacity
    full_in, full_out = (
        lax.all_gather(weight_in, "dp", axis=1, tiled=True),
        lax.all_gather(weight_out, "dp", axis=2, tiled=True),
    )
    full_in = full_in[0]
    full_out = full_out[0]
    flat_ids = route_ids.reshape(-1)
    onehot = (flat_ids[:, None] == jnp.arange(experts, dtype=jnp.int32)[None, :]).astype(jnp.int32)
    route_rank = jnp.sum(jnp.cumsum(onehot, axis=0) * onehot, axis=1) - 1
    slot_index = flat_ids * capacity + route_rank
    route_count = 2 * local_tokens
    route_of_slot = (
        jnp.full((slot_count,), route_count, jnp.int32)
        .at[slot_index]
        .set(jnp.arange(route_count, dtype=jnp.int32))
    )
    token_of_slot = route_of_slot // 2
    outbound_inputs = jnp.take(tokens, token_of_slot, axis=0, mode="fill", fill_value=0)
    outbound_grads = jnp.take(out_grad, token_of_slot, axis=0, mode="fill", fill_value=0)
    outbound_gates = jnp.take(
        route_gates.reshape(-1), route_of_slot, axis=0, mode="fill", fill_value=0
    )
    arrived_inputs, arrived_grads, arrived_gates = sent_together(
        (outbound_inputs, outbound_grads, outbound_gates), "expert", 0, 0, 1
    )
    preact, hidden_act = forward_rows(arrived_inputs, full_in)
    back_rows, back_gates, sum_in, sum_out = backward_rows(
        arrived_inputs, arrived_grads, arrived_gates, preact, hidden_act, full_in, full_out
    )
    home_grads, home_gates = sent_together(
        (back_rows, back_gates.astype(jnp.bfloat16)), "expert", 0, 0, 1
    )
    pair_rows = home_grads[slot_index].reshape(local_tokens, 2, model_width)
    grad_tokens = (
        pair_rows[:, 0].astype(jnp.float32) + pair_rows[:, 1].astype(jnp.float32)
    ).astype(jnp.bfloat16)
    grad_gates = home_gates[slot_index].reshape(local_tokens, 2)
    grad_weight_in, grad_weight_out = tuple(
        (
            part.astype(jnp.float32)
            for part in sum_together(
                (sum_in[None].astype(jnp.bfloat16), sum_out[None].astype(jnp.bfloat16)),
                "dp",
                (1, 2),
            )
        )
    )
    return (grad_tokens, grad_gates, grad_weight_in, grad_weight_out)


def solution(mesh):
    return jax.shard_map(
        on_device,
        mesh=mesh,
        in_specs=(
            P(("dp", "expert"), None),
            P(("dp", "expert"), None),
            P(("dp", "expert"), None),
            P(("dp", "expert"), None),
            P("expert", "dp", None),
            P("expert", None, "dp"),
        ),
        out_specs=(
            P(("dp", "expert"), None),
            P(("dp", "expert"), None),
            P("expert", "dp", None),
            P("expert", None, "dp"),
        ),
        check_vma=False,
    )
```

profile of v0, /device:TPU:8, one launch (start us, length us, event | category | flops | bytes accessed | tf_op | source)
XLA Modules:
  0.0 254.1 jit_solution(12017602975052510683)
XLA Ops:
  7.2 0.0 copy-start
  7.2 0.8 copy.26
  8.0 0.1 eq.29
  8.2 0.1 eq.25
  8.3 0.7 broadcast_multiply_fusion
  9.0 0.6 reduce-window.6
  9.6 0.2 slice_reduce_fusion.1
  9.8 0.1 fusion.14
  9.9 0.1 copy.25
  10.0 0.1 mul.58
  10.2 1.4 scatter_custom_fusion
  11.7 0.0 copy-done
  11.7 0.0 copy-start.1
  11.7 2.5 gather_fusion.3
  14.1 0.0 copy-done.1
  14.2 0.0 copy-start.3
  14.2 3.3 %gather_fusion.4 = bf16[512,2048]{1,0:T(8,128)(2,1)} fusion(bf16[128,2048]{1,0:T(8,128)(2,1)S(1)} %copy-done.1, s32[1024]{0:T(1024)S(1)} %pad_clamp_fusion.2), kind=kCustom, calls=%fused_computation.1.clone | custom fusion | bytes 4196352 | tf_op jit(solution)/shard_map/jit(_take)/gather | solution.py:94
  17.5 0.0 copy-done.3
  17.5 0.1 copy.29
  17.7 0.1 reshape.165
  17.8 3.4 %gather_fusion = bf16[512]{0:T(512)(128)(2,1)S(1)} fusion(bf16[256]{0:T(256)(128)(2,1)S(1)} %reshape.165, s32[1024]{0:T(1024)S(1)} %pad_clamp_fusion.1), kind=kCustom, calls=%fused_computation.2 | custom fusion | bytes 4096 | tf_op jit(solution)/shard_map/jit(_take)/gather | solution.py:95
  21.2 0.3 select_n.53
  21.5 1.9 broadcast_select_fusion.1
  23.4 2.2 pad_maximum_fusion
  25.6 13.3 %all-to-all-start = ((bf16[32,16,4097]{2,1,0:T(8,128)(2,1)}), bf16[32,16,4097]{2,1,0:T(8,128)(2,1)}, u32[]{:S(2)}, u32[]{:S(2)}) async-start(bf16[32,16,4097]{2,1,0:T(8,128)(2,1)} %pad_maximum_fusion), calls=%async_computation | async-start | bytes 8650752 | tf_op jit(solution)/shard_map/all_to_all | solution.py:14
  38.9 0.0 all-gather.3.cloned.1.call-start
  38.9 0.7 all-gather.3.cloned.1.call-update
  39.6 0.0 all-gather.5.cloned.1.call-start
  39.7 0.7 all-gather.5.cloned.1.call-update
  40.4 0.2 reduce-scatter.2.cloned.1.call-start
  40.6 95.3 %all-to-all-done = bf16[32,16,4097]{2,1,0:T(8,128)(2,1)} async-done(((bf16[32,16,4097]{2,1,0:T(8,128)(2,1)}), bf16[32,16,4097]{2,1,0:T(8,128)(2,1)}, u32[]{:S(2)}, u32[]{:S(2)}) %all-to-all-start) | async-done | bytes 4195360 | tf_op jit(solution)/shard_map/all_to_all | solution.py:14
  135.9 1.0 convert_reduce_fusion
  136.9 0.0 all-gather.3.cloned.1.call-done
  137.0 3.5 %fusion.3 = f32[512,512]{0,1:T(8,128)S(1)} fusion(bf16[1,512,2048]{2,1,0:T(8,128)(2,1)} %all-gather.3.cloned.1.call-done, bf16[512,4097]{1,0:T(8,128)(2,1)} %bitcast.5), kind=kOutput, calls=%fused_computation.18 | convolution fusion | flops 1073741824 | bytes 5242880 | tf_op jit(solution)/shard_map/dot_general | solution.py:52
  140.5 0.0 all-gather.5.cloned.1.call-done
  140.5 4.0 %multiply_convert_fusion.5 = (bf16[512,512]{0,1:T(8,128)(2,1)S(1)}, bf16[512]{0:T(512)(128)(2,1)S(1)}, f32[512,512]{0,1:T(8,128)S(1)}) fusion(f32[512,512]{0,1:T(8,128)S(1)} %fusion.3, f32[512]{0:T(512)S(1)} %convert_reduce_fusion, bf16[1,2048,512]{2,1,0:T(8,128)(2,1)} %all-gather.5.cloned.1.call-done, bf16[512,4097]{1,0:T(8,128)(2,1)} %bitcast.5), kind=kOutput, calls=%fused_computation.31 | convolution fusion | flops 1077673472 | bytes 6818816 | tf_op jit(solution)/shard_map/dot_general | solution.py:47
  144.5 3.0 %fusion.10 = bf16[64,8,16,128]{3,1,2,0:T(8,128)(2,1)S(1)} fusion(f32[512]{0:T(512)S(1)} %convert_reduce_fusion, bf16[512,4097]{1,0:T(8,128)(2,1)} %bitcast.5, f32[512,512]{0,1:T(8,128)S(1)} %get-tuple-element.23), kind=kOutput, calls=%fused_computation.27 | convolution fusion | flops 1079246848 | bytes 5244928 | tf_op jit(solution)/shard_map/dot_general | solution.py:65
  147.5 0.6 copy.39
  148.1 0.4 bitcast_bitcast_fusion
  148.5 0.5 copy.34
  149.0 1.4 copy.45
  150.4 4.2 %convolution_convert_fusion.1 = bf16[2048,512]{1,0:T(8,128)(2,1)} fusion(bf16[512,512]{0,1:T(8,128)(2,1)S(1)} %get-tuple-element.15, bf16[512,4097]{1,0:T(8,128)(2,1)} %bitcast.5), kind=kOutput, calls=%fused_computation.10 | convolution fusion | flops 1074790400 | bytes 4718592 | tf_op jit(solution)/shard_map/dot_general | solution.py:62
  154.6 3.2 %reshape_transpose_reshape.3 = bf16[16,65536]{1,0:T(8,128)(2,1)} reshape(bf16[2048,512]{1,0:T(8,128)(2,1)} %convolution_convert_fusion.1) | data formatting | bytes 4194304 | tf_op jit(solution)/shard_map/reshape;transpose;reshape | solution.py:30
  157.8 3.8 %pad_maximum_fusion.1 = bf16[16,131072]{1,0:T(8,128)(2,1)} fusion(bf16[16,65536]{1,0:T(8,128)(2,1)S(1)} %bitcast.59, bf16[16,65536]{1,0:T(8,128)(2,1)} %reshape_transpose_reshape.3), kind=kLoop, calls=%fused_computation.7 | loop fusion | flops 8388608 | bytes 8388608 | tf_op jit(solution)/shard_map/concatenate | solution.py:30
  161.7 4.8 %reshape.171 = bf16[16384,128]{1,0:T(8,128)(2,1)} reshape(bf16[16,131072]{1,0:T(8,128)(2,1)} %pad_maximum_fusion.1) | data formatting | bytes 8388608 | tf_op jit(solution)/shard_map/reshape | solution.py:32
  166.5 0.0 reduce-scatter.2.cloned.1.call-update
  166.5 0.3 convert_element_type.102
  166.8 2.9 %convolution_convert_fusion.2 = bf16[512,2048]{1,0:T(8,128)(2,1)S(1)} fusion(bf16[512,512]{0,1:T(8,128)(2,1)S(1)} %get-tuple-element.15, bf16[1,2048,512]{2,1,0:T(8,128)(2,1)} %all-gather.5.cloned.1.call-done), kind=kOutput, calls=%fused_computation.11 | convolution fusion | flops 1074790400 | bytes 4718592 | tf_op jit(solution)/shard_map/dot_general | solution.py:59
  169.7 1.6 pad_maximum_fusion.2
  171.2 7.1 %all-to-all-start.1 = ((bf16[32,16,2049]{2,1,0:T(8,128)(2,1)}), bf16[32,16,2049]{2,1,0:T(8,128)(2,1)S(1)}, u32[]{:S(2)}, u32[]{:S(2)}) async-start(bf16[32,16,2049]{2,1,0:T(8,128)(2,1)} %pad_maximum_fusion.2), calls=%async_computation.1 | async-start | bytes 4456448 | tf_op jit(solution)/shard_map/all_to_all | solution.py:14
  178.3 53.0 %all-to-all-done.1 = bf16[32,16,2049]{2,1,0:T(8,128)(2,1)S(1)} async-done(((bf16[32,16,2049]{2,1,0:T(8,128)(2,1)}), bf16[32,16,2049]{2,1,0:T(8,128)(2,1)S(1)}, u32[]{:S(2)}, u32[]{:S(2)}) %all-to-all-start.1) | async-done | bytes 2098208 | tf_op jit(solution)/shard_map/all_to_all | solution.py:14
  231.3 0.0 copy-start.2
  231.3 1.4 copy-done.2
  232.7 1.7 split.23
  234.4 2.4 gather_fusion.1
  236.8 1.7 reshape.166
  238.5 1.0 slice_reduce_fusion
  239.5 1.9 gather_fusion.2
  241.5 0.2 reshape.168
  241.6 0.6 copy.35
  242.2 1.5 fusion.20
  243.7 1.4 fusion.11
  245.1 1.7 fusion.12
  246.8 0.7 reshape.173
  (13 shorter events, 0.1 us)
Async XLA Ops:
  7.2 4.5 %copy-start = (bf16[128,2048]{1,0:T(8,128)(2,1)S(1)}, bf16[128,2048]{1,0:T(8,128)(2,1)}, u32[]{:S(2)}) copy-start(bf16[128,2048]{1,0:T(8,128)(2,1)} %param.8) | copy-start | bytes 1572868
  11.7 2.5 copy-start.1
  14.2 3.4 %copy-start.3 = (bf16[128,2]{0,1:T(2,128)(2,1)S(1)}, bf16[128,2]{0,1:T(2,128)(2,1)}, u32[]{:S(2)}) copy-start(bf16[128,2]{0,1:T(2,128)(2,1)} %param.11) | copy-start | bytes 1540
  25.6 110.3 %all-to-all-start = ((bf16[32,16,4097]{2,1,0:T(8,128)(2,1)}), bf16[32,16,4097]{2,1,0:T(8,128)(2,1)}, u32[]{:S(2)}, u32[]{:S(2)}) async-start(bf16[32,16,4097]{2,1,0:T(8,128)(2,1)} %pad_maximum_fusion), calls=%async_computation | async-start | bytes 8650752 | tf_op jit(solution)/shard_map/all_to_all | solution.py:14
  38.9 98.1 %all-gather.3.cloned.1.call-start = ((), (), s32[]{:S(2)}) async-start(), calls=%async_computation.3 | async-start | bytes 2228224 | tf_op jit(solution)/shard_map/all_gather | solution.py:78
  39.6 100.9 %all-gather.5.cloned.1.call-start = ((), (), s32[]{:S(2)}) async-start(), calls=%async_computation.4 | async-start | bytes 2228224 | tf_op jit(solution)/shard_map/all_gather | solution.py:77
  40.4 204.7 %reduce-scatter.2.cloned.1.call-start = ((), (), s32[]{:S(2)}) async-start(), calls=%async_computation.5 | async-start | bytes 4456448 | tf_op jit(solution)/shard_map/reduce_scatter | solution.py:33
  171.2 60.1 %all-to-all-start.1 = ((bf16[32,16,2049]{2,1,0:T(8,128)(2,1)}), bf16[32,16,2049]{2,1,0:T(8,128)(2,1)S(1)}, u32[]{:S(2)}, u32[]{:S(2)}) async-start(bf16[32,16,2049]{2,1,0:T(8,128)(2,1)} %pad_maximum_fusion.2), calls=%async_computation.1 | async-start | bytes 4456448 | tf_op jit(solution)/shard_map/all_to_all | solution.py:14
  231.3 1.4 copy-start.2
Sparse Core Ops, SparseCore 0:
  41.8 44.2 all-gather.2
  88.2 40.8 all-gather.4
  166.6 62.0 reduce-scatter.1
where the time goes:
time: 255 us; the launch traced here: 254 us
  waiting for transfers between devices  150 us (59%)
  local copies, waits for them, and re-layouts  37 us (15%)
  starting transfers between devices  20.6 us (8%)
  matrix products  17.6 us (7%)
  other arithmetic  15.1 us (6%)
  between operations  14 us (5%)
    all_to_all x2, waiting for transfers between devices, sent_together(): lax.all_to_all(both, axis, split_axis=split_dim, concat_axis=concat_dim,...  148 us
    all_to_all x2, starting transfers between devices, sent_together(): lax.all_to_all(both, axis, split_axis=split_dim, concat_axis=concat_dim,...  20.3 us
  transfers between devices with their start and end apart: 5, of which 2 were waited for; matrix products, arithmetic and copies ran while one was open for 9% of the time, Pallas kernels for 0%

commit v1 on v0

v1 whole, which is shorter than its diff:
```python
import jax
import jax.numpy as jnp
from jax import lax
from jax.experimental import pallas as pl
from jax.experimental.pallas import tpu as pltpu
from jax.sharding import PartitionSpec as P

NX, NY, NZ = 4, 8, 8
SLOTS = 16
LANES = 128
SUB = 32
TICKS = 12
VMEM = pltpu.VMEM
F32, BF16 = jnp.float32, jnp.bfloat16
PLUS, MINUS = 0, 1
BLOCKS = ((0, 128), (128, 128), (256, 96), (352, 32))
FORWARD = {0: 4, 1: 5, 2: 6, 3: 7, 4: 8, 5: 9, 6: 10, 8: 11}
BACKWARD_DEP = {after: before for before, after in FORWARD.items()}


def dot(a, b, dims):
    return lax.dot_general(a, b, (dims, ((), ())), preferred_element_type=F32)


def places():
    dp, ex = lax.axis_index("dp"), lax.axis_index("expert")
    return lax.div(dp, 2), lax.rem(dp, 2), lax.div(ex, NX), lax.rem(ex, NX)


def wrap(i, n):
    return lax.rem(i + n, n)


def device(y, c, z, x):
    return (y * 2 + c, z * NX + x)


def remote(src, dst, send, recv, to):
    return pltpu.make_async_remote_copy(
        src_ref=src, dst_ref=dst, send_sem=send, recv_sem=recv, device_id=to, device_id_type=pl.DeviceIdType.MESH
    )


def greet(y, c, z, x):
    peers = [device(y, c, wrap(z + d, NZ), x) for d in (1, -1)]
    peers += [device(y, c, z, lax.rem(x + d, NX)) for d in (1, 2, 3)]
    peers += [device(wrap(y + d, NY), c, z, x) for d in (1, -1)]
    peers += [device(y, 1 - c, z, x)]
    barrier = pltpu.get_barrier_semaphore()
    for peer in peers:
        pl.semaphore_signal(barrier, inc=1, device_id=peer, device_id_type=pl.DeviceIdType.MESH)
    pl.semaphore_wait(barrier, len(peers))


def prepare_kernel(tok, grad, ids, gates, own, plus, minus, perm_plus, perm_minus):
    n, width = tok.shape
    z = lax.div(lax.axis_index("expert"), NX)
    lane = lax.broadcasted_iota(jnp.int32, (n, LANES), 1)
    row = lax.broadcasted_iota(jnp.int32, (n, LANES), 0)
    before = (lane < row).astype(BF16)
    id0, id1 = ids[:, 0:1], ids[:, 1:2]
    g0, g1 = gates[:, 0:1].astype(F32), gates[:, 1:2].astype(F32)

    def pick(table, at):
        return jnp.sum(jnp.where(lane == at, table, 0.0), axis=1, keepdims=True)

    hit = ((lane == id0) | (lane == id1)).astype(BF16)
    earlier = dot(before, hit, ((1,), (0,)))
    rank0, rank1 = pick(earlier, id0), pick(earlier, id1)
    p0, p1 = lax.shift_right_logical(id0, 2), lax.shift_right_logical(id1, 2)
    hit_plane = ((lane == p0) | (lane == p1)).astype(F32)
    earlier_plane = dot(before, hit_plane.astype(BF16), ((1,), (0,)))
    far = lax.rem(z + 4, NZ)
    in_far = pick(hit_plane, far)
    far_rank = pick(earlier_plane, far)
    low = jnp.where(far_rank < 32.0, 1.0, 0.0)

    def table(i0, i1):
        out = jnp.zeros((n, LANES), F32)
        for k, col in enumerate((i0, i1, rank0, rank1, g0, g1)):
            out = jnp.where(lane == k, col, out)
        return out.astype(BF16)

    f0, f1 = id0.astype(F32), id1.astype(F32)
    both = jnp.concatenate([tok[...], grad[...]], axis=1)
    own[:, : 2 * width] = both
    own[:, 2 * width :] = table(f0, f1)
    for out, perm, mine, at in ((plus, perm_plus, low, lax.rem(z + 3, NZ)), (minus, perm_minus, 1.0 - low, lax.rem(z + 5, NZ))):
        first = in_far * mine
        second = pick(hit_plane, at) * (1.0 - first)
        third = 1.0 - first - second
        sets = jnp.where(lane == 0, first, jnp.where(lane == 1, second, jnp.where(lane == 2, third, 0.0)))
        ahead = dot(before, sets.astype(BF16), ((1,), (0,)))
        totals = jnp.sum(sets, axis=0, keepdims=True)
        n0 = jnp.sum(jnp.where(lane == 0, totals, 0.0), axis=1, keepdims=True)
        n1 = jnp.sum(jnp.where(lane == 1, totals, 0.0), axis=1, keepdims=True)
        place = first * pick(ahead, 0) + second * (n0 + pick(ahead, 1)) + third * (n0 + n1 + pick(ahead, 2))
        order = (lane.astype(F32) == place).astype(BF16)
        perm[...] = order
        drop = 1.0 - mine
        i0 = jnp.where((p0 == far) & (drop > 0.5), 64.0, f0)
        i1 = jnp.where((p1 == far) & (drop > 0.5), 64.0, f1)
        order_t = order.T
        out[:, : 2 * width] = dot(order_t, both, ((1,), (0,))).astype(BF16)
        out[:, 2 * width :] = dot(order_t, table(i0, i1), ((1,), (0,))).astype(BF16)


def prepare(tok, grad, ids, gates):
    n, width = tok.shape
    rows = jax.ShapeDtypeStruct((n, 2 * width + LANES), BF16)
    perm = jax.ShapeDtypeStruct((n, n), BF16)
    return pl.pallas_call(
        prepare_kernel,
        out_shape=(rows, rows, rows, perm, perm),
        in_specs=[pl.BlockSpec(memory_space=VMEM)] * 4,
        out_specs=(pl.BlockSpec(memory_space=VMEM),) * 5,
        name="prepare",
    )(tok, grad, ids, gates)


def match_table(columns, z):
    n = columns.shape[0]
    lane = lax.broadcasted_iota(jnp.int32, (n, NX * SLOTS), 1)
    expert = (z * NX + lax.div(lane, SLOTS)).astype(F32)
    rank = lax.rem(lane, SLOTS).astype(F32)
    c = columns.astype(F32)
    hit = ((c[:, 0:1] == expert) & (c[:, 2:3] == rank)) | ((c[:, 1:2] == expert) & (c[:, 3:4] == rank))
    return jnp.where(hit, 1.0, 0.0).astype(BF16)


def dispatch_kernel(own, plus, minus, w_in, w_out, slots, full_in, full_out, m_own, m_dirs,
                    arrived, staged, z_send, z_recv, x_send, x_recv, y_send, y_recv, c_send, c_recv):
    y, c, z, x = places()
    width = own.shape[1]
    data = width - LANES
    greet(y, c, z, x)
    source = (plus, minus)
    step = (1, -1)

    def z_copy(d, tick, src):
        return remote(src, arrived.at[d, pl.ds(SUB * tick, SUB)], z_send.at[d, tick], z_recv.at[d, tick],
                      device(y, c, wrap(z + step[d], NZ), x))

    for tick in range(4):
        for d in (PLUS, MINUS):
            z_copy(d, tick, source[d].at[pl.ds(SUB * tick, SUB)]).start()

    def in_slot(yy, cc):
        return full_in.at[pl.ds(pl.multiple_of((yy * 2 + cc) * 128, 128), 128), :]

    def out_slot(yy, cc):
        return full_out.at[:, pl.ds(pl.multiple_of((yy * 2 + cc) * 128, 128), 128)]

    slot_of = (in_slot, out_slot)
    shard = (w_in, w_out)
    parts = {(d, h): (0, 1) for d in (0, 1) for h in (1, 2, 3)}
    parts[(0, 4)], parts[(1, 4)] = (0,), (1,)

    def y_copy(d, hop, part, src):
        origin = wrap(y - step[d] * (hop - 1) + NY, NY)
        return remote(src, slot_of[part](origin, c), y_send.at[d, hop - 1, part], y_recv.at[d, hop - 1, part],
                      device(wrap(y + step[d], NY), c, z, x))

    def c_copy(k, part, origin, src):
        return remote(src, slot_of[part](origin, c), c_send.at[k, part], c_recv.at[k, part], device(y, 1 - c, z, x))

    for part in (0, 1):
        for d in (0, 1):
            y_copy(d, 1, part, shard[part]).start()
        c_copy(0, part, y, shard[part]).start()
    in_slot(y, c)[...] = w_in[...]
    out_slot(y, c)[...] = w_out[...]

    def partner_index(d, hop):
        return 7 if hop == 4 else 3 * d + hop

    def y_step(hop):
        for d in (0, 1):
            origin = wrap(y - step[d] * hop + NY, NY)
            for part in parts[(d, hop)]:
                here = slot_of[part](origin, c)
                remote(here, here, y_send.at[d, hop - 1, part], y_recv.at[d, hop - 1, part],
                       device(wrap(y + step[d], NY), c, z, x)).wait_recv()
                if part in parts.get((d, hop + 1), ()):
                    y_copy(d, hop + 1, part, here).start()
                c_copy(partner_index(d, hop), part, origin, here).start()

    def x_copy(k, dx, origin_z):
        to = lax.rem(x + dx, NX)
        return remote(
            staged.at[k, pl.ds(pl.multiple_of(to * SLOTS, SLOTS), SLOTS)],
            slots.at[pl.ds(pl.multiple_of((origin_z * NX + x) * SLOTS, SLOTS), SLOTS)],
            x_send.at[k, dx - 1], x_recv.at[k, dx - 1], device(y, c, z, to))

    def send_selected(k, origin_z):
        for dx in (1, 3, 2):
            x_copy(k, dx, origin_z).start()
        mine = staged[k, pl.ds(pl.multiple_of(x * SLOTS, SLOTS), SLOTS), :]
        slots[pl.ds(pl.multiple_of((origin_z * NX + x) * SLOTS, SLOTS), SLOTS), :] = mine

    m0 = match_table(own[:, data:], z)
    m_own[...] = m0
    staged[0] = dot(m0, own[...], ((0,), (0,))).astype(BF16)
    send_selected(0, z)

    def origin_of(d, hop):
        return wrap(z - step[d] * hop + NZ, NZ)

    def select(d, hop):
        at, n = BLOCKS[hop - 1]
        m = match_table(arrived[d, at : at + n, data:], z)
        m_dirs[d, at : at + n] = m
        return dot(m, arrived[d, at : at + n, :], ((0,), (0,)))

    for tick in range(TICKS):
        for d in (PLUS, MINUS):
            here = arrived.at[d, pl.ds(SUB * tick, SUB)]
            z_copy(d, tick, here).wait_recv()
            if tick in FORWARD:
                z_copy(d, FORWARD[tick], here).start()
        if tick < 4:
            y_step(tick + 1)
        hop = {3: 1, 7: 2, 10: 3}.get(tick)
        if hop:
            for d in (PLUS, MINUS):
                k = 2 * hop - 1 + d
                staged[k] = select(d, hop).astype(BF16)
                send_selected(k, origin_of(d, hop))
    staged[7] = (select(PLUS, 4) + select(MINUS, 4)).astype(BF16)
    send_selected(7, origin_of(PLUS, 4))

    order = [(0, z)] + [(2 * h - 1 + d, origin_of(d, h)) for h in (1, 2, 3) for d in (0, 1)] + [(7, origin_of(0, 4))]
    for k, origin_z in order:
        for dx in (1, 2, 3):
            sender = lax.rem(x + NX - dx, NX)
            there = slots.at[pl.ds(pl.multiple_of((origin_z * NX + sender) * SLOTS, SLOTS), SLOTS)]
            remote(there, there, x_send.at[k, dx - 1], x_recv.at[k, dx - 1],
                   device(y, c, z, sender)).wait_recv()
            x_copy(k, dx, origin_z).wait_send()
    for k, origin, which in ([(0, y, (0, 1))]
                             + [(3 * d + h, wrap(y - step[d] * h + NY, NY), (0, 1)) for d in (0, 1) for h in (1, 2, 3)]
                             + [(7, wrap(y + 4, NY), (0, 1))]):
        for part in which:
            there = slot_of[part](origin, 1 - c)
            remote(there, there, c_send.at[k, part], c_recv.at[k, part], device(y, 1 - c, z, x)).wait_recv()
            src = shard[part] if k == 0 else slot_of[part](origin, c)
            c_copy(k, part, origin, src).wait_send()
    for (d, hop), which in parts.items():
        for part in which:
            origin = wrap(y - step[d] * (hop - 1) + NY, NY)
            src = shard[part] if hop == 1 else slot_of[part](origin, c)
            y_copy(d, hop, part, src).wait_send()
    back = {after: before for before, after in FORWARD.items()}
    for tick in range(TICKS):
        for d in (PLUS, MINUS):
            if tick < 4:
                src = source[d].at[pl.ds(SUB * tick, SUB)]
            else:
                src = arrived.at[d, pl.ds(SUB * back[tick], SUB)]
            z_copy(d, tick, src).wait_send()


def dispatch(own, plus, minus, w_in, w_out):
    width = own.shape[1]
    experts = NX * NZ
    hidden = w_in.shape[1]
    model = w_in.shape[0] * 2 * NY
    dma = pltpu.SemaphoreType.DMA
    return pl.pallas_call(
        dispatch_kernel,
        out_shape=(
            jax.ShapeDtypeStruct((experts * SLOTS, width), BF16),
            jax.ShapeDtypeStruct((model, hidden), BF16),
            jax.ShapeDtypeStruct((hidden, model), BF16),
            jax.ShapeDtypeStruct((own.shape[0], NX * SLOTS), BF16),
            jax.ShapeDtypeStruct((2, SUB * TICKS, NX * SLOTS), BF16),
        ),
        in_specs=[pl.BlockSpec(memory_space=VMEM)] * 5,
        out_specs=(pl.BlockSpec(memory_space=VMEM),) * 5,
        scratch_shapes=[
            VMEM((2, SUB * TICKS, width), BF16),
            VMEM((8, NX * SLOTS, width), BF16),
            dma((2, TICKS)), dma((2, TICKS)),
            dma((8, 3)), dma((8, 3)),
            dma((2, 4, 2)), dma((2, 4, 2)),
            dma((8, 2)), dma((8, 2)),
        ],
        compiler_params=pltpu.CompilerParams(collective_id=0, has_side_effects=True),
        name="dispatch",
    )(own, plus, minus, w_in, w_out)


def experts_kernel(slots, full_in, full_out, results, part_in, part_out, pre_grad, hidden_act, scaled):
    rows, width = slots.shape
    model, hidden = full_in.shape
    ex = lax.axis_index("expert").astype(F32)
    chunk = 128

    def forward(i, _):
        at = pl.ds(pl.multiple_of(i * chunk, chunk), chunk)
        columns = slots[at, 2 * model :].astype(F32)
        first = columns[:, 0:1] == ex
        gate = jnp.where(first, columns[:, 4:5], columns[:, 5:6])
        grad = slots[at, model : 2 * model]
        preact = dot(slots[at, :model], full_in[...], ((1,), (0,)))
        back = dot(grad, full_out[...], ((1,), (1,)))
        s = jax.nn.sigmoid(preact)
        act = (preact * s).astype(BF16)
        hidden_act[at, :] = act
        gate_grad = jnp.sum(act.astype(F32) * back, axis=1, keepdims=True)
        pre = (gate * back * (s * (1.0 + preact * (1.0 - s)))).astype(BF16)
        pre_grad[at, :] = pre
        scaled[at, :] = (gate * grad.astype(F32)).astype(BF16)
        results[at, :model] = dot(pre, full_in[...], ((1,), (1,))).astype(BF16)
        lane = lax.broadcasted_iota(jnp.int32, (chunk, LANES), 1)
        column = jnp.where(first, 0, 1)
        results[at, model:] = jnp.where(lane == column, gate_grad, 0.0).astype(BF16)
        return 0

    lax.fori_loop(0, rows // chunk, forward, 0)

    for k in range(model // 512):
        term = dot(slots[:, 512 * k : 512 * (k + 1)], pre_grad[...], ((0,), (0,))).astype(BF16)
        for j in range(4):
            dp = 4 * k + j
            part_in[dp % 2, dp // 2] = term[128 * j : 128 * (j + 1), :]
        term = dot(hidden_act[...], scaled[:, 512 * k : 512 * (k + 1)], ((0,), (0,))).astype(BF16)
        for j in range(4):
            dp = 4 * k + j
            part_out[dp % 2, dp // 2] = term[:, 128 * j : 128 * (j + 1)]


def run_experts(slots, full_in, full_out):
    rows = slots.shape[0]
    model, hidden = full_in.shape
    share = model // (2 * NY)
    return pl.pallas_call(
        experts_kernel,
        out_shape=(
            jax.ShapeDtypeStruct((rows, model + LANES), BF16),
            jax.ShapeDtypeStruct((2, NY, share, hidden), BF16),
            jax.ShapeDtypeStruct((2, NY, hidden, share), BF16),
        ),
        in_specs=[pl.BlockSpec(memory_space=VMEM)] * 3,
        out_specs=(pl.BlockSpec(memory_space=VMEM),) * 3,
        scratch_shapes=[VMEM((rows, hidden), BF16), VMEM((rows, hidden), BF16), VMEM((rows, model), BF16)],
        name="experts",
    )(slots, full_in, full_out)


def collect_kernel(results, part_in, part_out, m_own, m_dirs, perm_plus, perm_minus,
                   grad_tokens, grad_gates, grad_in, grad_out,
                   gathered, outgoing, arrived, partner_in, partner_out, sum_in, sum_out, got_in, got_out,
                   z_send, z_recv, x_send, x_recv, y_send, y_recv, c_send, c_recv):
    y, c, z, x = places()
    model = grad_tokens.shape[1]
    greet(y, c, z, x)
    step = (1, -1)
    partner = device(y, 1 - c, z, x)
    mine_t, partner_t, sum_t, got_t = (part_in, part_out), (partner_in, partner_out), (sum_in, sum_out), (got_in, got_out)

    def origin_of(d, hop):
        return wrap(z - step[d] * hop + NZ, NZ)

    planes = [(7, origin_of(0, 4))] + [(2 * h - 1 + d, origin_of(d, h)) for h in (3, 2, 1) for d in (0, 1)] + [(0, z)]

    def x_copy(k, dx, origin_z):
        to = lax.rem(x + dx, NX)
        return remote(
            results.at[pl.ds(pl.multiple_of((origin_z * NX + to) * SLOTS, SLOTS), SLOTS)],
            gathered.at[k, pl.ds(pl.multiple_of(x * SLOTS, SLOTS), SLOTS)],
            x_send.at[k, dx - 1], x_recv.at[k, dx - 1], device(y, c, z, to))

    for k, origin_z in planes:
        for dx in (1, 3, 2):
            x_copy(k, dx, origin_z).start()

    def c_copy(part):
        return remote(mine_t[part].at[1 - c], partner_t[part], c_send.at[part], c_recv.at[part], partner)

    for part in (0, 1):
        c_copy(part).start()
    for k, origin_z in planes:
        at = pl.ds(pl.multiple_of(x * SLOTS, SLOTS), SLOTS)
        gathered[k, at, :] = results[pl.ds(pl.multiple_of((origin_z * NX + x) * SLOTS, SLOTS), SLOTS), :]

    def x_wait(k):
        for dx in (1, 2, 3):
            sender = lax.rem(x + NX - dx, NX)
            there = gathered.at[k, pl.ds(pl.multiple_of(sender * SLOTS, SLOTS), SLOTS)]
            remote(there, there, x_send.at[k, dx - 1], x_recv.at[k, dx - 1], device(y, c, z, sender)).wait_recv()

    def z_copy(d, tick):
        at = pl.ds(SUB * tick, SUB)
        return remote(outgoing.at[d, at], arrived.at[d, at], z_send.at[d, tick], z_recv.at[d, tick],
                      device(y, c, wrap(z - step[d], NZ), x))

    def z_step(tick, hop):
        for d in (PLUS, MINUS):
            k = 7 if hop == 4 else 2 * hop - 1 + d
            rows = dot(m_dirs[d, SUB * tick : SUB * (tick + 1), :], gathered[k], ((1,), (0,)))
            later = FORWARD.get(tick)
            if later is not None:
                z_copy(d, later).wait_recv()
                rows = rows + arrived[d, SUB * later : SUB * (later + 1), :].astype(F32)
            outgoing[d, SUB * tick : SUB * (tick + 1), :] = rows.astype(BF16)
            z_copy(d, tick).start()

    y_parts = {(d, h): (0, 1) for d in (0, 1) for h in (1, 2, 3)}
    y_parts[(0, 4)], y_parts[(1, 4)] = (0,), (1,)

    def y_copy(d, hop, part):
        return remote(sum_t[part].at[d, hop - 1], got_t[part].at[d, hop - 1], y_send.at[d, hop - 1, part],
                      y_recv.at[d, hop - 1, part], device(wrap(y - step[d], NY), c, z, x))

    def y_step(hop):
        for d in (0, 1):
            target = wrap(y - step[d] * hop + NY, NY)
            for part in y_parts[(d, hop)]:
                total = mine_t[part][c, target].astype(F32) + partner_t[part][target].astype(F32)
                if part in y_parts.get((d, hop + 1), ()):
                    y_copy(d, hop + 1, part).wait_recv()
                    total = total + got_t[part][d, hop].astype(F32)
                sum_t[part][d, hop - 1] = total.astype(BF16)
                y_copy(d, hop, part).start()

    x_wait(7)
    z_step(11, 4)
    for part in (0, 1):
        c_copy(part).wait_recv()
    y_step(4)
    x_wait(5)
    x_wait(6)
    z_step(9, 3)
    z_step(10, 3)
    z_step(8, 3)
    y_step(3)
    x_wait(3)
    x_wait(4)
    z_step(7, 2)
    z_step(5, 2)
    z_step(6, 2)
    z_step(4, 2)
    y_step(2)
    x_wait(1)
    x_wait(2)
    z_step(1, 1)
    z_step(2, 1)
    y_step(1)
    z_step(0, 1)
    z_step(3, 1)
    x_wait(0)
    total = dot(m_own[...], gathered[0], ((1,), (0,)))
    for part, out in ((0, grad_in), (1, grad_out)):
        acc = mine_t[part][c, y].astype(F32) + partner_t[part][y].astype(F32)
        for d in (0, 1):
            y_copy(d, 1, part).wait_recv()
            acc = acc + got_t[part][d, 0].astype(F32)
        out[...] = acc
    for tick in (1, 2, 0, 3):
        for d in (PLUS, MINUS):
            z_copy(d, tick).wait_recv()
    for d, perm in ((PLUS, perm_plus), (MINUS, perm_minus)):
        total = total + dot(perm[...], arrived[d, 0:128, :], ((1,), (0,)))
    grad_tokens[...] = total[:, :model].astype(BF16)
    grad_gates[...] = total[:, model : model + 2].astype(BF16)

    for k, origin_z in planes:
        for dx in (1, 2, 3):
            x_copy(k, dx, origin_z).wait_send()
    for part in (0, 1):
        c_copy(part).wait_send()
    for (d, hop), which in y_parts.items():
        for part in which:
            y_copy(d, hop, part).wait_send()
    for tick in range(TICKS):
        for d in (PLUS, MINUS):
            z_copy(d, tick).wait_send()


def collect(results, part_in, part_out, m_own, m_dirs, perm_plus, perm_minus):
    width = results.shape[1]
    model = width - LANES
    n = m_own.shape[0]
    _, _, share, hidden = part_in.shape
    dma = pltpu.SemaphoreType.DMA
    shard_in, shard_out = (share, hidden), (hidden, share)
    return pl.pallas_call(
        collect_kernel,
        out_shape=(
            jax.ShapeDtypeStruct((n, model), BF16),
            jax.ShapeDtypeStruct((n, 2), BF16),
            jax.ShapeDtypeStruct(shard_in, F32),
            jax.ShapeDtypeStruct(shard_out, F32),
        ),
        in_specs=[pl.BlockSpec(memory_space=VMEM)] * 7,
        out_specs=(pl.BlockSpec(memory_space=VMEM),) * 4,
        scratch_shapes=[
            VMEM((8, NX * SLOTS, width), BF16),
            VMEM((2, SUB * TICKS, width), BF16),
            VMEM((2, SUB * TICKS, width), BF16),
            VMEM((NY,) + shard_in, BF16), VMEM((NY,) + shard_out, BF16),
            VMEM((2, 4) + shard_in, BF16), VMEM((2, 4) + shard_out, BF16),
            VMEM((2, 4) + shard_in, BF16), VMEM((2, 4) + shard_out, BF16),
            dma((2, TICKS)), dma((2, TICKS)),
            dma((8, 3)), dma((8, 3)),
            dma((2, 4, 2)), dma((2, 4, 2)),
            dma((2,)), dma((2,)),
        ],
        compiler_params=pltpu.CompilerParams(collective_id=1, has_side_effects=True),
        name="collect",
    )(results, part_in, part_out, m_own, m_dirs, perm_plus, perm_minus)


def on_device(tokens, out_grad, route_ids, route_gates, weight_in, weight_out):
    own, plus, minus, perm_plus, perm_minus = prepare(tokens, out_grad, route_ids, route_gates)
    slots, full_in, full_out, m_own, m_dirs = dispatch(own, plus, minus, weight_in[0], weight_out[0])
    results, part_in, part_out = run_experts(slots, full_in, full_out)
    grad_tokens, grad_gates, grad_in, grad_out = collect(
        results, part_in, part_out, m_own, m_dirs, perm_plus, perm_minus
    )
    return grad_tokens, grad_gates, grad_in[None], grad_out[None]


def solution(mesh):
    rows = P(("dp", "expert"), None)
    return jax.shard_map(
        on_device,
        mesh=mesh,
        in_specs=(rows, rows, rows, rows, P("expert", "dp", None), P("expert", None, "dp")),
        out_specs=(rows, rows, P("expert", "dp", None), P("expert", None, "dp")),
        check_vma=False,
    )
```

time: 255 us -> 185 us (0.73)
  the two profiles are of different devices: /device:TPU:8 before, /device:TPU:2 now
where the time goes in v1:
time: 185 us
  Pallas kernels  175 us (95%)
  local copies, waits for them, and re-layouts  9.37 us (5%)
    pallas_call x1, Pallas kernels, dispatch(): pl.pallas_call(dispatch_kernel, out_shape=(jax.ShapeDtypeStruct((experts...  104 us
    pallas_call x1, Pallas kernels, collect(): pl.pallas_call(collect_kernel, out_shape=(jax.ShapeDtypeStruct((n, model)...  51.6 us
    pallas_call x1, Pallas kernels, run_experts(): pl.pallas_call(experts_kernel, out_shape=(jax.ShapeDtypeStruct((rows, mod...  15.1 us
    unnamed x6, local copies, waits for them, and re-layouts  9.37 us
    pallas_call x1, Pallas kernels, prepare(): pl.pallas_call(prepare_kernel, out_shape=(rows, rows, rows, perm, perm),...  4.27 us

profile of v1, /device:TPU:2, one launch (start us, length us, event | category | flops | bytes accessed | tf_op | source)
XLA Modules:
  0.0 185.0 jit_solution(16996382777422668473)
XLA Ops:
  0.6 1.4 copy.11.gates
  2.0 1.4 copy.10.ids
  3.4 4.3 %prepare.1 = (bf16[128,4224]{1,0:T(8,128)(2,1)}, bf16[128,4224]{1,0:T(8,128)(2,1)}, bf16[128,4224]{1,0:T(8,128)(2,1)}, bf16[128,128]{1,0:T(8,128)(2,1)}, bf16[128,128]{1,0:T(8,128)(2,1)}) custom-call(bf16[128,2048]{1,0:T(8,128)(2,1)} %tok.1, bf16[128,2048]{1,0:T(8,128)(2,1)} %grad.1, s32[128,2]{1,0:T(8,128)} %copy.10.ids, bf16[128,2]{1,0:T(8,128)(2,1)} %copy.11.gates), custom_call_target="tpu_custom_call" | custom-call | tf_op jit(solution)/shard_map/prepare/pallas_call | solution.py:112
  7.7 104.1 %dispatch.1 = (bf16[512,4224]{1,0:T(8,128)(2,1)}, bf16[2048,512]{1,0:T(8,128)(2,1)}, bf16[512,2048]{1,0:T(8,128)(2,1)}, bf16[128,64]{1,0:T(8,128)(2,1)}, bf16[2,384,64]{2,1,0:T(8,128)(2,1)}) custom-call(bf16[128,4224]{1,0:T(8,128)(2,1)} %get-tuple-element.21.own, bf16[128,4224]{1,0:T(8,128)(2,1)} %get-tuple-element.22.plus, ...), custom_call_target="tpu_custom_call" | custom-call | tf_op jit(solution)/shard_map/dispatch/pallas_call | solution.py:269
  111.8 15.1 %experts.1 = (bf16[512,2176]{1,0:T(8,128)(2,1)}, bf16[2,8,128,512]{3,2,1,0:T(8,128)(2,1)}, bf16[2,8,512,128]{3,2,1,0:T(8,128)(2,1)}) custom-call(bf16[512,4224]{1,0:T(8,128)(2,1)} %get-tuple-element.24.slots, bf16[2048,512]{1,0:T(8,128)(2,1)} %get-tuple-element.25.full_in, bf16[512,2048]{1,0:T(8,128)(2,1)} %get-tuple-element.26.full_out), custom_call_target="tpu_custom_call" | custom-call | tf_op jit(solution)/shard_map/experts/pallas_call | solution.py:337
  126.9 51.6 %collect.1 = (bf16[128,2048]{1,0:T(8,128)(2,1)}, bf16[128,2]{1,0:T(8,128)(2,1)}, f32[128,512]{1,0:T(8,128)}, f32[512,128]{1,0:T(8,128)}) custom-call(bf16[512,2176]{1,0:T(8,128)(2,1)} %get-tuple-element.27.results, bf16[2,8,128,512]{3,2,1,0:T(8,128)(2,1)} %get-tuple-element.28.part_in, bf16[2,8,512,128]{3,2,1,0:T(8,128)(2,1)} %get-tuple-element.29.part_out, ...), custom_call_target="tpu_custom_call" | custom-call | tf_op jit(solution)/shard_map/collect/pallas_call | solution.py:488
  178.5 1.4 copy.12
  179.8 1.9 %copy.16 = bf16[128,2048]{1,0:T(8,128)(2,1)} copy(bf16[128,2048]{1,0:T(8,128)(2,1)} %get-tuple-element.46) | data formatting | bytes 1048576
  181.7 1.7 copy.17
  183.4 1.7 copy.18

commit v2 on v1

--- a/solution.py
+++ b/solution.py
@@ -41,6 +41,10 @@
     )
 
 
+def via(k):
+    return NX - 1 if k % 2 else 1
+
+
 def greet(y, c, z, x):
     peers = [device(y, c, wrap(z + d, NZ), x) for d in (1, -1)]
     peers += [device(y, c, z, lax.rem(x + d, NX)) for d in (1, 2, 3)]
@@ -58,8 +62,9 @@
     lane = lax.broadcasted_iota(jnp.int32, (n, LANES), 1)
     row = lax.broadcasted_iota(jnp.int32, (n, LANES), 0)
     before = (lane < row).astype(BF16)
-    id0, id1 = ids[:, 0:1], ids[:, 1:2]
-    g0, g1 = gates[:, 0:1].astype(F32), gates[:, 1:2].astype(F32)
+    columns = jnp.concatenate([ids[...].astype(F32), gates[...].astype(F32), jnp.zeros((4, n), F32)], axis=0).T
+    f0, f1, g0, g1 = (columns[:, k : k + 1] for k in range(4))
+    id0, id1 = f0.astype(jnp.int32), f1.astype(jnp.int32)
 
     def pick(table, at):
         return jnp.sum(jnp.where(lane == at, table, 0.0), axis=1, keepdims=True)
@@ -81,7 +86,6 @@
             out = jnp.where(lane == k, col, out)
         return out.astype(BF16)
 
-    f0, f1 = id0.astype(F32), id1.astype(F32)
     both = jnp.concatenate([tok[...], grad[...]], axis=1)
     own[:, : 2 * width] = both
     own[:, 2 * width :] = table(f0, f1)
@@ -129,7 +133,8 @@
 
 
 def dispatch_kernel(own, plus, minus, w_in, w_out, slots, full_in, full_out, m_own, m_dirs,
-                    arrived, staged, z_send, z_recv, x_send, x_recv, y_send, y_recv, c_send, c_recv):
+                    arrived, staged, passing, z_send, z_recv, x_send, x_recv, p_send, p_recv,
+                    y_send, y_recv, c_send, c_recv):
     y, c, z, x = places()
     width = own.shape[1]
     data = width - LANES
@@ -185,15 +190,28 @@
                     y_copy(d, hop + 1, part, here).start()
                 c_copy(partner_index(d, hop), part, origin, here).start()
 
+    def slot_rows(origin_z, origin_x):
+        return slots.at[pl.ds(pl.multiple_of((origin_z * NX + origin_x) * SLOTS, SLOTS), SLOTS)]
+
     def x_copy(k, dx, origin_z):
         to = lax.rem(x + dx, NX)
-        return remote(
-            staged.at[k, pl.ds(pl.multiple_of(to * SLOTS, SLOTS), SLOTS)],
-            slots.at[pl.ds(pl.multiple_of((origin_z * NX + x) * SLOTS, SLOTS), SLOTS)],
-            x_send.at[k, dx - 1], x_recv.at[k, dx - 1], device(y, c, z, to))
+        src = staged.at[k, pl.ds(pl.multiple_of(to * SLOTS, SLOTS), SLOTS)]
+        if dx == 2:
+            return remote(src, passing.at[k], x_send.at[k, 1], x_recv.at[k, 1],
+                          device(y, c, z, lax.rem(x + via(k), NX)))
+        return remote(src, slot_rows(origin_z, x), x_send.at[k, dx - 1], x_recv.at[k, dx - 1], device(y, c, z, to))
+
+    def pass_copy(k, origin_z):
+        return remote(passing.at[k], slot_rows(origin_z, lax.rem(x + NX - via(k), NX)), p_send.at[k], p_recv.at[k],
+                      device(y, c, z, lax.rem(x + via(k), NX)))
+
+    def pass_on(k, origin_z):
+        remote(passing.at[k], passing.at[k], x_send.at[k, 1], x_recv.at[k, 1],
+               device(y, c, z, lax.rem(x + NX - via(k), NX))).wait_recv()
+        pass_copy(k, origin_z).start()
 
     def send_selected(k, origin_z):
-        for dx in (1, 3, 2):
+        for dx in (2, 1, 3):
             x_copy(k, dx, origin_z).start()
         mine = staged[k, pl.ds(pl.multiple_of(x * SLOTS, SLOTS), SLOTS), :]
         slots[pl.ds(pl.multiple_of((origin_z * NX + x) * SLOTS, SLOTS), SLOTS), :] = mine
@@ -220,6 +238,12 @@
                 z_copy(d, FORWARD[tick], here).start()
         if tick < 4:
             y_step(tick + 1)
+        if tick == 1:
+            pass_on(0, z)
+        if tick in (5, 9):
+            for d in (PLUS, MINUS):
+                hop = 1 if tick == 5 else 2
+                pass_on(2 * hop - 1 + d, origin_of(d, hop))
         hop = {3: 1, 7: 2, 10: 3}.get(tick)
         if hop:
             for d in (PLUS, MINUS):
@@ -228,15 +252,22 @@
                 send_selected(k, origin_of(d, hop))
     staged[7] = (select(PLUS, 4) + select(MINUS, 4)).astype(BF16)
     send_selected(7, origin_of(PLUS, 4))
+    for d in (PLUS, MINUS):
+        pass_on(5 + d, origin_of(d, 3))
+    pass_on(7, origin_of(PLUS, 4))
 
     order = [(0, z)] + [(2 * h - 1 + d, origin_of(d, h)) for h in (1, 2, 3) for d in (0, 1)] + [(7, origin_of(0, 4))]
     for k, origin_z in order:
-        for dx in (1, 2, 3):
+        for dx in (1, 3):
             sender = lax.rem(x + NX - dx, NX)
-            there = slots.at[pl.ds(pl.multiple_of((origin_z * NX + sender) * SLOTS, SLOTS), SLOTS)]
+            there = slot_rows(origin_z, sender)
             remote(there, there, x_send.at[k, dx - 1], x_recv.at[k, dx - 1],
                    device(y, c, z, sender)).wait_recv()
+        there = slot_rows(origin_z, lax.rem(x + 2, NX))
+        remote(there, there, p_send.at[k], p_recv.at[k], device(y, c, z, lax.rem(x + NX - via(k), NX))).wait_recv()
+        for dx in (1, 2, 3):
             x_copy(k, dx, origin_z).wait_send()
+        pass_copy(k, origin_z).wait_send()
     for k, origin, which in ([(0, y, (0, 1))]
                              + [(3 * d + h, wrap(y - step[d] * h + NY, NY), (0, 1)) for d in (0, 1) for h in (1, 2, 3)]
                              + [(7, wrap(y + 4, NY), (0, 1))]):
@@ -280,8 +311,10 @@
         scratch_shapes=[
             VMEM((2, SUB * TICKS, width), BF16),
             VMEM((8, NX * SLOTS, width), BF16),
+            VMEM((8, SLOTS, width), BF16),
             dma((2, TICKS)), dma((2, TICKS)),
             dma((8, 3)), dma((8, 3)),
+            dma((8,)), dma((8,)),
             dma((2, 4, 2)), dma((2, 4, 2)),
             dma((8, 2)), dma((8, 2)),
         ],
@@ -348,12 +381,11 @@
     )(slots, full_in, full_out)
 
 
-def collect_kernel(results, part_in, part_out, m_own, m_dirs, perm_plus, perm_minus,
-                   grad_tokens, grad_gates, grad_in, grad_out,
-                   gathered, outgoing, arrived, partner_in, partner_out, sum_in, sum_out, got_in, got_out,
-                   z_send, z_recv, x_send, x_recv, y_send, y_recv, c_send, c_recv):
+def collect_kernel(results, part_in, part_out, m_own, m_dirs,
+                   back, grad_in, grad_out,
+                   gathered, passing, outgoing, arrived, partner_in, partner_out, sum_in, sum_out, got_in, got_out,
+                   z_send, z_recv, x_send, x_recv, p_send, p_recv, y_send, y_recv, c_send, c_recv):
     y, c, z, x = places()
-    model = grad_tokens.shape[1]
     greet(y, c, z, x)
     step = (1, -1)
     partner = device(y, 1 - c, z, x)
@@ -362,37 +394,56 @@
     def origin_of(d, hop):
         return wrap(z - step[d] * hop + NZ, NZ)
 
-    planes = [(7, origin_of(0, 4))] + [(2 * h - 1 + d, origin_of(d, h)) for h in (3, 2, 1) for d in (0, 1)] + [(0, z)]
-
-    def x_copy(k, dx, origin_z):
+    plane_of = {7: origin_of(0, 4), 0: z}
+    for h in (1, 2, 3):
+        for d in (0, 1):
+            plane_of[2 * h - 1 + d] = origin_of(d, h)
+
+    def gathered_rows(k, origin_x):
+        return gathered.at[k, pl.ds(pl.multiple_of(origin_x * SLOTS, SLOTS), SLOTS)]
+
+    def x_copy(k, dx):
         to = lax.rem(x + dx, NX)
-        return remote(
-            results.at[pl.ds(pl.multiple_of((origin_z * NX + to) * SLOTS, SLOTS), SLOTS)],
-            gathered.at[k, pl.ds(pl.multiple_of(x * SLOTS, SLOTS), SLOTS)],
-            x_send.at[k, dx - 1], x_recv.at[k, dx - 1], device(y, c, z, to))
-
-    for k, origin_z in planes:
-        for dx in (1, 3, 2):
-            x_copy(k, dx, origin_z).start()
+        src = results.at[pl.ds(pl.multiple_of((plane_of[k] * NX + to) * SLOTS, SLOTS), SLOTS)]
+        if dx == 2:
+            return remote(src, passing.at[k], x_send.at[k, 1], x_recv.at[k, 1],
+                          device(y, c, z, lax.rem(x + via(k), NX)))
+        return remote(src, gathered_rows(k, x), x_send.at[k, dx - 1], x_recv.at[k, dx - 1], device(y, c, z, to))
+
+    def pass_copy(k):
+        return remote(passing.at[k], gathered_rows(k, lax.rem(x + NX - via(k), NX)), p_send.at[k], p_recv.at[k],
+                      device(y, c, z, lax.rem(x + via(k), NX)))
+
+    def x_start(*ks):
+        for k in ks:
+            for dx in (2, 1, 3):
+                x_copy(k, dx).start()
+            at = pl.ds(pl.multiple_of(x * SLOTS, SLOTS), SLOTS)
+            gathered[k, at, :] = results[pl.ds(pl.multiple_of((plane_of[k] * NX + x) * SLOTS, SLOTS), SLOTS), :]
+
+    def pass_on(*ks):
+        for k in ks:
+            remote(passing.at[k], passing.at[k], x_send.at[k, 1], x_recv.at[k, 1],
+                   device(y, c, z, lax.rem(x + NX - via(k), NX))).wait_recv()
+            pass_copy(k).start()
 
     def c_copy(part):
         return remote(mine_t[part].at[1 - c], partner_t[part], c_send.at[part], c_recv.at[part], partner)
 
-    for part in (0, 1):
-        c_copy(part).start()
-    for k, origin_z in planes:
-        at = pl.ds(pl.multiple_of(x * SLOTS, SLOTS), SLOTS)
-        gathered[k, at, :] = results[pl.ds(pl.multiple_of((origin_z * NX + x) * SLOTS, SLOTS), SLOTS), :]
-
-    def x_wait(k):
-        for dx in (1, 2, 3):
-            sender = lax.rem(x + NX - dx, NX)
-            there = gathered.at[k, pl.ds(pl.multiple_of(sender * SLOTS, SLOTS), SLOTS)]
-            remote(there, there, x_send.at[k, dx - 1], x_recv.at[k, dx - 1], device(y, c, z, sender)).wait_recv()
+    def x_wait(*ks):
+        for k in ks:
+            for dx in (1, 3):
+                sender = lax.rem(x + NX - dx, NX)
+                there = gathered_rows(k, sender)
+                remote(there, there, x_send.at[k, dx - 1], x_recv.at[k, dx - 1], device(y, c, z, sender)).wait_recv()
+            there = gathered_rows(k, lax.rem(x + 2, NX))
+            remote(there, there, p_send.at[k], p_recv.at[k],
+                   device(y, c, z, lax.rem(x + NX - via(k), NX))).wait_recv()
 
     def z_copy(d, tick):
         at = pl.ds(SUB * tick, SUB)
-        return remote(outgoing.at[d, at], arrived.at[d, at], z_send.at[d, tick], z_recv.at[d, tick],
+        dst = back.at[d, at] if tick < 4 else arrived.at[d, at]
+        return remote(outgoing.at[d, at], dst, z_send.at[d, tick], z_recv.at[d, tick],
                       device(y, c, wrap(z - step[d], NZ), x))
 
     def z_step(tick, hop):
@@ -424,33 +475,41 @@
                 sum_t[part][d, hop - 1] = total.astype(BF16)
                 y_copy(d, hop, part).start()
 
+    x_start(7, 5)
+    for part in (0, 1):
+        c_copy(part).start()
+    pass_on(7)
+    x_start(6, 3)
     x_wait(7)
     z_step(11, 4)
+    pass_on(5, 6)
+    x_start(4, 1)
     for part in (0, 1):
         c_copy(part).wait_recv()
     y_step(4)
-    x_wait(5)
-    x_wait(6)
+    x_wait(5, 6)
     z_step(9, 3)
     z_step(10, 3)
+    pass_on(3, 4)
+    x_start(2, 0)
     z_step(8, 3)
     y_step(3)
-    x_wait(3)
-    x_wait(4)
+    x_wait(3, 4)
     z_step(7, 2)
+    pass_on(1, 2)
     z_step(5, 2)
     z_step(6, 2)
     z_step(4, 2)
+    pass_on(0)
     y_step(2)
-    x_wait(1)
-    x_wait(2)
+    x_wait(1, 2)
     z_step(1, 1)
     z_step(2, 1)
     y_step(1)
     z_step(0, 1)
     z_step(3, 1)
     x_wait(0)
-    total = dot(m_own[...], gathered[0], ((1,), (0,)))
+    back[2] = dot(m_own[...], gathered[0], ((1,), (0,))).astype(BF16)
     for part, out in ((0, grad_in), (1, grad_out)):
         acc = mine_t[part][c, y].astype(F32) + partner_t[part][y].astype(F32)
         for d in (0, 1):
@@ -460,14 +519,11 @@
     for tick in (1, 2, 0, 3):
         for d in (PLUS, MINUS):
             z_copy(d, tick).wait_recv()
-    for d, perm in ((PLUS, perm_plus), (MINUS, perm_minus)):
-        total = total + dot(perm[...], arrived[d, 0:128, :], ((1,), (0,)))
-    grad_tokens[...] = total[:, :model].astype(BF16)
-    grad_gates[...] = total[:, model : model + 2].astype(BF16)
-
-    for k, origin_z in planes:
+
+    for k in range(8):
         for dx in (1, 2, 3):
-            x_copy(k, dx, origin_z).wait_send()
+            x_copy(k, dx).wait_send()
+        pass_copy(k).wait_send()
     for part in (0, 1):
         c_copy(part).wait_send()
     for (d, hop), which in y_parts.items():
@@ -478,9 +534,8 @@
             z_copy(d, tick).wait_send()
 
 
-def collect(results, part_in, part_out, m_own, m_dirs, perm_plus, perm_minus):
+def collect(results, part_in, part_out, m_own, m_dirs):
     width = results.shape[1]
-    model = width - LANES
     n = m_own.shape[0]
     _, _, share, hidden = part_in.shape
     dma = pltpu.SemaphoreType.DMA
@@ -488,15 +543,15 @@
     return pl.pallas_call(
         collect_kernel,
         out_shape=(
-            jax.ShapeDtypeStruct((n, model), BF16),
-            jax.ShapeDtypeStruct((n, 2), BF16),
+            jax.ShapeDtypeStruct((3, n, width), BF16),
             jax.ShapeDtypeStruct(shard_in, F32),
             jax.ShapeDtypeStruct(shard_out, F32),
         ),
-        in_specs=[pl.BlockSpec(memory_space=VMEM)] * 7,
-        out_specs=(pl.BlockSpec(memory_space=VMEM),) * 4,
+        in_specs=[pl.BlockSpec(memory_space=VMEM)] * 5,
+        out_specs=(pl.BlockSpec(memory_space=VMEM),) * 3,
         scratch_shapes=[
             VMEM((8, NX * SLOTS, width), BF16),
+            VMEM((8, SLOTS, width), BF16),
             VMEM((2, SUB * TICKS, width), BF16),
             VMEM((2, SUB * TICKS, width), BF16),
             VMEM((NY,) + shard_in, BF16), VMEM((NY,) + shard_out, BF16),
@@ -504,22 +559,49 @@
             VMEM((2, 4) + shard_in, BF16), VMEM((2, 4) + shard_out, BF16),
             dma((2, TICKS)), dma((2, TICKS)),
             dma((8, 3)), dma((8, 3)),
+            dma((8,)), dma((8,)),
             dma((2, 4, 2)), dma((2, 4, 2)),
             dma((2,)), dma((2,)),
         ],
         compiler_params=pltpu.CompilerParams(collective_id=1, has_side_effects=True),
         name="collect",
-    )(results, part_in, part_out, m_own, m_dirs, perm_plus, perm_minus)
+    )(results, part_in, part_out, m_own, m_dirs)
+
+
+def finish_kernel(back, perm_plus, perm_minus, sum_in, sum_out, grad_tokens, grad_gates, grad_in, grad_out):
+    model = grad_tokens.shape[1]
+    total = back[2].astype(F32)
+    for d, perm in ((PLUS, perm_plus), (MINUS, perm_minus)):
+        total = total + dot(perm[...], back[d], ((1,), (0,)))
+    grad_tokens[...] = total[:, :model].astype(BF16)
+    grad_gates[...] = total[:, model:].T[0:2, :].astype(BF16)
+    grad_in[...] = sum_in[...]
+    grad_out[...] = sum_out[...]
+
+
+def finish(back, perm_plus, perm_minus, sum_in, sum_out):
+    _, n, width = back.shape
+    return pl.pallas_call(
+        finish_kernel,
+        out_shape=(
+            jax.ShapeDtypeStruct((n, width - LANES), BF16),
+            jax.ShapeDtypeStruct((2, n), BF16),
+            jax.ShapeDtypeStruct(sum_in.shape, F32),
+            jax.ShapeDtypeStruct(sum_out.shape, F32),
+        ),
+        in_specs=[pl.BlockSpec(memory_space=VMEM)] * 5,
+        out_specs=(pl.BlockSpec(memory_space=VMEM),) * 4,
+        name="finish",
+    )(back, perm_plus, perm_minus, sum_in, sum_out)
 
 
 def on_device(tokens, out_grad, route_ids, route_gates, weight_in, weight_out):
-    own, plus, minus, perm_plus, perm_minus = prepare(tokens, out_grad, route_ids, route_gates)
+    own, plus, minus, perm_plus, perm_minus = prepare(tokens, out_grad, route_ids.T, route_gates.T)
     slots, full_in, full_out, m_own, m_dirs = dispatch(own, plus, minus, weight_in[0], weight_out[0])
     results, part_in, part_out = run_experts(slots, full_in, full_out)
-    grad_tokens, grad_gates, grad_in, grad_out = collect(
-        results, part_in, part_out, m_own, m_dirs, perm_plus, perm_minus
-    )
-    return grad_tokens, grad_gates, grad_in[None], grad_out[None]
+    back, sum_in, sum_out = collect(results, part_in, part_out, m_own, m_dirs)
+    grad_tokens, grad_gates, grad_in, grad_out = finish(back, perm_plus, perm_minus, sum_in, sum_out)
+    return grad_tokens, grad_gates.T, grad_in[None], grad_out[None]
 
 
 def solution(mesh):

time: 185 us -> 186 us (level)
  Pallas kernels: 175 us -> 185 us
  local copies, waits for them, and re-layouts: 9.37 us -> 0 us
    unnamed x6 -> x0, local copies, waits for them, and re-layouts: 9.37 us -> none
    pallas_call x1 -> x2, Pallas kernels: 51.6 us -> 58.8 us  [the longest x1 55.8 us: collect(): pl.pallas_call(collect_kernel, out_shape=(jax.ShapeDtypeStruct((3, n, wid...]
    pallas_call x1, Pallas kernels: 104 us -> 106 us  [dispatch(): pl.pallas_call(dispatch_kernel, out_shape=(jax.ShapeDtypeStruct((experts...]
where the time goes in v2:
time: 186 us; the launch traced here: 185 us
  Pallas kernels  185 us (99%)
    pallas_call x1, Pallas kernels, dispatch(): pl.pallas_call(dispatch_kernel, out_shape=(jax.ShapeDtypeStruct((experts...  106 us
    pallas_call x1, Pallas kernels, collect(): pl.pallas_call(collect_kernel, out_shape=(jax.ShapeDtypeStruct((3, n, wid...  55.8 us
    pallas_call x1, Pallas kernels, run_experts(): pl.pallas_call(experts_kernel, out_shape=(jax.ShapeDtypeStruct((rows, mod...  15.1 us
    pallas_call x1, Pallas kernels, prepare(): pl.pallas_call(prepare_kernel, out_shape=(rows, rows, rows, perm, perm),...  4.41 us

profile of v2, /device:TPU:2, one launch (start us, length us, event | category | flops | bytes accessed | tf_op | source)
XLA Modules:
  0.0 185.4 jit_solution(14934048415479005542)
XLA Ops:
  0.6 4.4 %prepare.1 = (bf16[128,4224]{1,0:T(8,128)(2,1)}, bf16[128,4224]{1,0:T(8,128)(2,1)}, bf16[128,4224]{1,0:T(8,128)(2,1)}, bf16[128,128]{1,0:T(8,128)(2,1)}, bf16[128,128]{1,0:T(8,128)(2,1)}) custom-call(bf16[128,2048]{1,0:T(8,128)(2,1)} %tok.1, bf16[128,2048]{1,0:T(8,128)(2,1)} %grad.1, s32[2,128]{1,0:T(2,128)} %bitcast.9, bf16[2,128]{1,0:T(2,128)(2,1)} %bitcast.10), custom_call_target="tpu_custom_call" | custom-call | tf_op jit(solution)/shard_map/prepare/pallas_call | solution.py:116
  5.0 106.5 %dispatch.1 = (bf16[512,4224]{1,0:T(8,128)(2,1)}, bf16[2048,512]{1,0:T(8,128)(2,1)}, bf16[512,2048]{1,0:T(8,128)(2,1)}, bf16[128,64]{1,0:T(8,128)(2,1)}, bf16[2,384,64]{2,1,0:T(8,128)(2,1)}) custom-call(bf16[128,4224]{1,0:T(8,128)(2,1)} %get-tuple-element.24.own, bf16[128,4224]{1,0:T(8,128)(2,1)} %get-tuple-element.25.plus, ...), custom_call_target="tpu_custom_call" | custom-call | tf_op jit(solution)/shard_map/dispatch/pallas_call | solution.py:300
  111.5 15.1 %experts.1 = (bf16[512,2176]{1,0:T(8,128)(2,1)}, bf16[2,8,128,512]{3,2,1,0:T(8,128)(2,1)}, bf16[2,8,512,128]{3,2,1,0:T(8,128)(2,1)}) custom-call(bf16[512,4224]{1,0:T(8,128)(2,1)} %get-tuple-element.27.slots, bf16[2048,512]{1,0:T(8,128)(2,1)} %get-tuple-element.28.full_in, bf16[512,2048]{1,0:T(8,128)(2,1)} %get-tuple-element.29.full_out), custom_call_target="tpu_custom_call" | custom-call | tf_op jit(solution)/shard_map/experts/pallas_call | solution.py:370
  126.7 55.8 %collect.1 = (bf16[3,128,2176]{2,1,0:T(8,128)(2,1)}, f32[128,512]{1,0:T(8,128)}, f32[512,128]{1,0:T(8,128)}) custom-call(bf16[512,2176]{1,0:T(8,128)(2,1)} %get-tuple-element.30.results, bf16[2,8,128,512]{3,2,1,0:T(8,128)(2,1)} %get-tuple-element.31.part_in, bf16[2,8,512,128]{3,2,1,0:T(8,128)(2,1)} %get-tuple-element.32.part_out, ...), custom_call_target="tpu_custom_call" | custom-call | tf_op jit(solution)/shard_map/collect/pallas_call | solution.py:543
  182.5 3.0 %finish.1 = (bf16[128,2048]{1,0:T(8,128)(2,1)}, bf16[2,128]{1,0:T(2,128)(2,1)}, f32[128,512]{1,0:T(8,128)}, f32[512,128]{1,0:T(8,128)}) custom-call(bf16[3,128,2176]{2,1,0:T(8,128)(2,1)} %get-tuple-element.35.back, bf16[128,128]{1,0:T(8,128)(2,1)} %get-tuple-element.36.perm_plus, bf16[128,128]{1,0:T(8,128)(2,1)} %get-tuple-element.37.perm_minus, ...), custom_call_target="tpu_custom_call" | custom-call | tf_op jit(solution)/shard_map/finish/pallas_call | solution.py:584
